TPU v7x, 32 devices: a whole 2x2x4 slice. The times are simulated.
32 devices in a mesh: visit: 8 (over y, x, core), sky: 4 (over z).
Axes of the slice: x: 2, y: 2, z: 4, core: 2. Of those that a mesh axis runs over, the one named last changes fastest.
Arguments:
- science: float32 [8, 16, 128, 128], P('visit', 'sky'), may hold values from -6 to 6
- coef_first: float32 [8, 16, 3, 49], P('visit', 'sky'), may hold values from -4 to 4
- coef_second: float32 [8, 16, 3, 49], P('visit', 'sky'), may hold values from -4 to 4
- weight: float32 [8, 16], P('visit', 'sky'), may hold values from 0.3 to 3
- slot_tile: int32 [8, 16], P('visit', 'sky'), may hold values from 0 to 3, as said below
- offsets: int32 [8, 16, 2], P('visit', 'sky'), may hold values from 0 to 128
- counts: int32 [8, 4], P('visit', 'sky'), may hold values from 3 to 4, as said below
- tile_place: int32 [4], replicated, may hold values from 0 to 3, as said below
Outputs:
- template: float32 [4, 256, 256], P('sky')
- difference: float32 [8, 16, 128, 128], P('visit', 'sky')
Inputs may be any that keep to these rules, and one draw needn't show every extreme that they name: `slot_tile`: among the usable slots of one device's list at most 2 name tiles of one owner; in every visit the tile of some owner gets exactly 2 usable slots from every device of the sky axis. A permutation: tile t is owned by the device of sky index tile_place[t]. The first counts[v, s] slots of a device's list are usable; in every visit some device has all 4 usable.
All inputs are finite; a program needn't handle non-finite values.
Results may differ from a plain program's by a relative error of at most 0.00011.
Values sent between devices are 32-bit elements; how exact they have to be, the bound alone decides.
No kernel may reach another device: no remote copies, remote signals or barrier semaphores. Data moves between devices by JAX's collectives and lax.ppermute only.
A program may use at most 64 MiB of HBM per device.

v0:
```python
import jax
import jax.numpy as jnp
from jax import lax
from jax.sharding import PartitionSpec as P

TILE = 256
TAPS = 21
PROFILES = 7
WIDTHS = (1.0, 1.0, 1.0, 2.5, 2.5, 2.5, 5.0)
POWERS = (0, 1, 2, 0, 1, 2, 0)
PRECISE = lax.Precision.HIGHEST


def profile_filters(side):
    reach = (TAPS - 1) // 2
    places = jnp.arange(side).astype(jnp.float32)
    spacing = places[None, :] - places[:, None]
    support = jnp.arange(TAPS).astype(jnp.float32) - reach
    stacked = []
    for number in range(PROFILES):
        sample = support ** POWERS[number] * jnp.exp(
            -support * support / (2.0 * WIDTHS[number] ** 2)
        )
        norming = jnp.sqrt(jnp.sum(sample * sample))
        values = spacing ** POWERS[number] * jnp.exp(
            -spacing * spacing / (2.0 * WIDTHS[number] ** 2)
        )
        stacked.append(jnp.where(jnp.abs(spacing) <= reach, values / norming, 0.0))
    return jnp.stack(stacked)


def positions(side):
    places = jnp.arange(side).astype(jnp.float32)
    return (2.0 * places - (side - 1)) / (side - 1)


def kernel_pass(block, coeffs, filters, spread):
    across_x = jnp.einsum("yw,ixw->iyx", block, filters, precision=PRECISE)
    layout = coeffs.reshape(3, PROFILES, PROFILES)
    plain = jnp.einsum("ij,jab->iab", layout[0], filters, precision=PRECISE)
    along = jnp.einsum("ij,jab->iab", layout[2], filters, precision=PRECISE) * spread[None, :, None]
    sideways = jnp.einsum("ij,jab->iab", layout[1], filters, precision=PRECISE)
    steady = jnp.einsum("iab,ibx->ax", plain + along, across_x, precision=PRECISE)
    varying = jnp.einsum("iab,ibx->ax", sideways, across_x, precision=PRECISE)
    return steady + varying * spread[None, :]


def body(science, coef_first, coef_second, weight, slot_tile, offsets, counts, tile_place):
    slots = science.shape[1]
    side = science.shape[2]
    owners_count = lax.axis_size("sky")
    capacity = max(2, (slots + owners_count - 1) // owners_count)
    buffer_slots = owners_count * capacity
    filters = profile_filters(side)
    spread = positions(side)
    listed = jnp.arange(slots)
    usable = listed < counts[0, 0]
    tile_ids = jnp.arange(tile_place.shape[0])
    owners = jnp.sum(
        jnp.where(slot_tile[0][:, None] == tile_ids[None, :], tile_place[None, :], 0), axis=1
    )
    convolved = lax.map(
        lambda operands: kernel_pass(operands[0], operands[1], filters, spread),
        (science[0], coef_first[0]),
    )
    sharing = (
        (owners[:, None] == owners[None, :]) & usable[None, :] & (listed[None, :] < listed[:, None])
    )
    earlier = jnp.sum(sharing.astype(jnp.int32), axis=1)
    target = jnp.where(usable, owners * capacity + earlier, -1)
    routing = (target[None, :] == jnp.arange(buffer_slots)[:, None]).astype(jnp.float32)
    packed = jnp.dot(routing, convolved.reshape(slots, side * side), precision=PRECISE).reshape(
        buffer_slots, side, side
    )
    sent_weight = jnp.dot(routing, weight[0], precision=PRECISE)
    sent_corner = jnp.dot(routing, offsets[0].astype(jnp.float32), precision=PRECISE)
    arrived, arrived_weight, arrived_corner = (
        lax.all_to_all(packed, "sky", split_axis=0, concat_axis=0, tiled=True),
        lax.all_to_all(sent_weight, "sky", split_axis=0, concat_axis=0, tiled=True),
        lax.all_to_all(sent_corner, "sky", split_axis=0, concat_axis=0, tiled=True),
    )
    corners = arrived_corner.astype(jnp.int32)

    def place_block(position, totals):
        weighted, coverage = totals
        corner_top = corners[position, 0]
        corner_left = corners[position, 1]
        block_weight = arrived_weight[position]
        region = lax.dynamic_slice(weighted, (corner_top, corner_left), (side, side))
        weighted = lax.dynamic_update_slice(
            weighted, region + block_weight * arrived[position], (corner_top, corner_left)
        )
        region = lax.dynamic_slice(coverage, (corner_top, corner_left), (side, side))
        coverage = lax.dynamic_update_slice(
            coverage, region + block_weight, (corner_top, corner_left)
        )
        return (weighted, coverage)

    empty = jnp.zeros((TILE, TILE), jnp.float32)
    weighted, coverage = lax.fori_loop(0, buffer_slots, place_block, (empty, empty))
    weighted, coverage = lax.psum((weighted, coverage), "visit")
    template = weighted / (coverage + 1.0)
    cut_back = jax.vmap(
        lambda corner: lax.dynamic_slice(template, (corner[0], corner[1]), (side, side))
    )(corners)
    returned = lax.all_to_all(cut_back, "sky", split_axis=0, concat_axis=0, tiled=True)
    cutouts = jnp.dot(
        routing.T, returned.reshape(buffer_slots, side * side), precision=PRECISE
    ).reshape(slots, side, side)
    matched = lax.map(
        lambda operands: kernel_pass(operands[0], operands[1], filters, spread),
        (cutouts, coef_second[0]),
    )
    difference = jnp.where(usable[:, None, None], science[0] - matched, 0.0)
    return (template[None], difference[None])


def solution(mesh):
    in_specs = (
        P("visit", "sky", None, None),
        P("visit", "sky", None, None),
        P("visit", "sky", None, None),
        P("visit", "sky"),
        P("visit", "sky"),
        P("visit", "sky", None),
        P("visit", "sky"),
        P(),
    )
    out_specs = (P("sky", None, None), P("visit", "sky", None, None))
    return jax.shard_map(body, mesh=mesh, in_specs=in_specs, out_specs=out_specs, check_vma=False)
```

profile of v0, /device:TPU:0, one launch (start us, length us, event | category | flops | bytes accessed | tf_op | source)
XLA Modules:
  0.0 270.1 jit_solution(13443177923790171623)
XLA Ops:
  9.8 6.3 %all-to-all-start.1 = ((f32[4,2,1]{1,2,0:T(1,128)}), f32[4,2,1]{1,2,0:T(1,128)S(1)}, u32[]{:S(2)}, u32[]{:S(2)}) async-start(f32[4,2,1]{1,2,0:T(1,128)} %copy.57), calls=%async_computation.1 | async-start | bytes 4096 | tf_op jit(solution)/shard_map/all_to_all | solution.py:79
  26.9 0.9 copy-done.4
  27.8 15.7 %while.42 = (s32[]{:T(128)}, f32[4,128,128]{2,1,0:T(8,128)S(1)}, f32[4,3,49]{2,1,0:T(4,128)S(1)}, f32[7,128,128]{2,0,1:T(8,128)S(1)}, f32[4,128,128]{2,1,0:T(8,128)S(1)}, /*index=5*/s32[]{:T(128)}) while((s32[]{:T(128)}, f32[4,128,128]{2,1,0:T(8,128)S(1)}, f32[4,3,49]{2,1,0:T(4,128)S(1)}, ...), condition=%wide.region_10.11_spmd.clone.clone, body=%wide.region_9.10_spmd.clone.clone.sunk | while | flops 557646336 | bytes 6362725 | solution.py:62
  45.0 5.1 %all-to-all-start = ((f32[4,2,2]{2,1,0:T(2,128)}), f32[4,2,2]{2,1,0:T(2,128)S(1)}, u32[]{:S(2)}, u32[]{:S(2)}) async-start(f32[4,2,2]{2,1,0:T(2,128)} %fusion.28), calls=%async_computation | async-start | bytes 8192 | tf_op jit(solution)/shard_map/all_to_all | solution.py:80
  50.1 0.9 copy.59
  51.0 4.7 %all-to-all-done = f32[4,2,2]{2,1,0:T(2,128)S(1)} async-done(((f32[4,2,2]{2,1,0:T(2,128)}), f32[4,2,2]{2,1,0:T(2,128)S(1)}, u32[]{:S(2)}, u32[]{:S(2)}) %all-to-all-start) | async-done | bytes 96 | tf_op jit(solution)/shard_map/all_to_all | solution.py:80
  55.6 3.5 %all-to-all-start.2 = ((f32[8,128,128]{2,1,0:T(8,128)}), f32[8,128,128]{2,1,0:T(8,128)S(1)}, u32[]{:S(2)}, u32[]{:S(2)}) async-start(f32[8,128,128]{2,1,0:T(8,128)} %copy.59), calls=%async_computation.2 | async-start | bytes 1048576 | tf_op jit(solution)/shard_map/all_to_all | solution.py:78
  60.7 11.1 %all-to-all-done.2 = f32[8,128,128]{2,1,0:T(8,128)S(1)} async-done(((f32[8,128,128]{2,1,0:T(8,128)}), f32[8,128,128]{2,1,0:T(8,128)S(1)}, u32[]{:S(2)}, u32[]{:S(2)}) %all-to-all-start.2) | async-done | bytes 524320 | tf_op jit(solution)/shard_map/all_to_all | solution.py:78
  71.9 77.3 %while.40 = (s32[]{:T(128)}, f32[256,256]{1,0:T(8,128)S(1)}, f32[256,256]{1,0:T(8,128)S(1)}, s32[8,2]{0,1:T(2,128)S(1)}, f32[8]{0:T(128)S(1)}, /*index=5*/f32[8,...) while((s32[]{:T(128)}, f32[256,256]{1,0:T(8,128)S(1)}, f32[256,256]{1,0:T(8,128)S(1)}, ...), condition=%wide.region_12.13_spmd, body=%wide.region_11.12_spmd.sunk | while | flops 49160 | bytes 591569 | solution.py:100
  77.2 0.8 bitcast_add_fusion.2
  78.0 2.0 dynamic_update_slice.32
  79.9 2.0 dynamic_update_slice.31
  87.2 0.8 bitcast_add_fusion.2
  88.0 1.9 dynamic_update_slice.32
  89.9 1.9 dynamic_update_slice.31
  97.2 0.8 bitcast_add_fusion.2
  97.9 2.0 dynamic_update_slice.32
  99.9 2.0 dynamic_update_slice.31
  107.2 0.8 bitcast_add_fusion.2
  107.9 1.7 dynamic_update_slice.32
  109.6 1.7 dynamic_update_slice.31
  116.6 0.8 bitcast_add_fusion.2
  117.3 1.9 dynamic_update_slice.32
  119.2 1.9 dynamic_update_slice.31
  126.4 0.8 bitcast_add_fusion.2
  127.1 1.7 dynamic_update_slice.32
  128.8 1.7 dynamic_update_slice.31
  135.8 0.8 bitcast_add_fusion.2
  136.5 1.7 dynamic_update_slice.32
  138.2 1.7 dynamic_update_slice.31
  145.1 0.8 bitcast_add_fusion.2
  145.9 1.7 dynamic_update_slice.32
  147.6 1.7 dynamic_update_slice.31
  150.1 54.8 %all-reduce.3.cloned.1.call-done = (f32[256,256]{1,0:T(8,128)}, f32[256,256]{1,0:T(8,128)}) async-done(((f32[256,256]{1,0:T(8,128)}, f32[256,256]{1,0:T(8,128)}), (f32[256,256]{1,0:T(8,128)}, f32[256,256]{1,0:T(8,128)})) %all-reduce.3.cloned.1.call-update) | async-done | bytes 524304 | tf_op jit(solution)/shard_map/psum | solution.py:101
  204.9 1.1 add_divide_fusion
  205.9 20.8 %while.41 = (s32[]{:T(128)}, f32[256,256]{1,0:T(8,128)S(1)}, s32[8,2]{0,1:T(2,128)S(1)}, f32[8,128,128]{2,1,0:T(8,128)}, s32[]{:T(128)}) while((s32[]{:T(128)}, f32[256,256]{1,0:T(8,128)S(1)}, s32[8,2]{0,1:T(2,128)S(1)}, f32[8,128,128]{2,1,0:T(8,128)}, s32[]{:T(128)}) %tuple.118), condition=%wide.while_cond, body=%wide.while_body.sunk | while | flops 2 | bytes 132705 | solution.py:104
  206.6 2.0 bitcast_dynamic-update-slice_fusion.2
  209.2 2.0 bitcast_dynamic-update-slice_fusion.2
  211.8 2.0 bitcast_dynamic-update-slice_fusion.2
  214.4 2.0 bitcast_dynamic-update-slice_fusion.2
  217.0 2.0 bitcast_dynamic-update-slice_fusion.2
  219.5 2.0 bitcast_dynamic-update-slice_fusion.2
  222.2 2.0 bitcast_dynamic-update-slice_fusion.2
  224.8 2.0 bitcast_dynamic-update-slice_fusion.2
  227.5 4.6 %all-to-all-start.3 = ((f32[8,128,128]{2,1,0:T(8,128)}), f32[8,128,128]{2,1,0:T(8,128)S(1)}, u32[]{:S(2)}, u32[]{:S(2)}) async-start(f32[8,128,128]{2,1,0:T(8,128)} %get-tuple-element.193), calls=%async_computation.3 | async-start | bytes 1048576 | tf_op jit(solution)/shard_map/all_to_all | solution.py:106
  232.0 13.8 %all-to-all-done.3 = f32[8,128,128]{2,1,0:T(8,128)S(1)} async-done(((f32[8,128,128]{2,1,0:T(8,128)}), f32[8,128,128]{2,1,0:T(8,128)S(1)}, u32[]{:S(2)}, u32[]{:S(2)}) %all-to-all-start.3) | async-done | bytes 524320 | tf_op jit(solution)/shard_map/all_to_all | solution.py:106
  246.5 16.0 %while.43 = (s32[]{:T(128)}, f32[4,128,128]{2,1,0:T(8,128)S(1)}, f32[4,3,49]{2,1,0:T(4,128)S(1)}, f32[7,128,128]{2,0,1:T(8,128)S(1)}, f32[4,128,128]{2,0,1:T(4,128)S(1)}, /*index=5*/s32[]{:T(128)}) while((s32[]{:T(128)}, f32[4,128,128]{2,1,0:T(8,128)S(1)}, f32[4,3,49]{2,1,0:T(4,128)S(1)}, ...), condition=%wide.region_16.17_spmd.clone.clone, body=%wide.region_15.16_spmd.clone.clone.sunk | while | flops 557646336 | bytes 6428261 | solution.py:110
  262.5 0.8 select_bitcast_fusion
  (191 shorter events, 59.2 us)
Async XLA Ops:
  7.2 1.8 copy-start
  7.8 0.7 copy-start.8
  7.9 0.7 copy-start.9
  9.8 35.1 %all-to-all-start.1 = ((f32[4,2,1]{1,2,0:T(1,128)}), f32[4,2,1]{1,2,0:T(1,128)S(1)}, u32[]{:S(2)}, u32[]{:S(2)}) async-start(f32[4,2,1]{1,2,0:T(1,128)} %copy.57), calls=%async_computation.1 | async-start | bytes 4096 | tf_op jit(solution)/shard_map/all_to_all | solution.py:79
  22.7 2.7 %copy-start.5 = (f32[1,4,3,49]{3,1,2,0:T(4,128)S(1)}, f32[1,4,3,49]{3,1,2,0:T(4,128)}, u32[]{:S(2)}) copy-start(f32[1,4,3,49]{3,1,2,0:T(4,128)} %param.15) | copy-start | bytes 7060
  26.8 1.0 copy-start.4
  43.5 0.7 copy-start.7
  45.0 10.7 %all-to-all-start = ((f32[4,2,2]{2,1,0:T(2,128)}), f32[4,2,2]{2,1,0:T(2,128)S(1)}, u32[]{:S(2)}, u32[]{:S(2)}) async-start(f32[4,2,2]{2,1,0:T(2,128)} %fusion.28), calls=%async_computation | async-start | bytes 8192 | tf_op jit(solution)/shard_map/all_to_all | solution.py:80
  55.6 16.2 %all-to-all-start.2 = ((f32[8,128,128]{2,1,0:T(8,128)}), f32[8,128,128]{2,1,0:T(8,128)S(1)}, u32[]{:S(2)}, u32[]{:S(2)}) async-start(f32[8,128,128]{2,1,0:T(8,128)} %copy.59), calls=%async_computation.2 | async-start | bytes 1048576 | tf_op jit(solution)/shard_map/all_to_all | solution.py:78
  59.1 145.8 %all-reduce.3.cloned.1.call-start = ((), (), s32[]{:S(2)}) async-start(), calls=%async_computation.4 | async-start | bytes 1048576 | tf_op jit(solution)/shard_map/psum | solution.py:101
  149.2 0.7 copy-start.1
  149.3 0.8 copy-start.2
  226.8 0.7 copy-start.3
  226.8 5.3 %copy-start.6 = (f32[1,4,3,49]{3,1,2,0:T(4,128)S(1)}, f32[1,4,3,49]{3,1,2,0:T(4,128)}, u32[]{:S(2)}) copy-start(f32[1,4,3,49]{3,1,2,0:T(4,128)} %param.16) | copy-start | bytes 7060
  227.5 18.3 %all-to-all-start.3 = ((f32[8,128,128]{2,1,0:T(8,128)}), f32[8,128,128]{2,1,0:T(8,128)S(1)}, u32[]{:S(2)}, u32[]{:S(2)}) async-start(f32[8,128,128]{2,1,0:T(8,128)} %get-tuple-element.193), calls=%async_computation.3 | async-start | bytes 1048576 | tf_op jit(solution)/shard_map/all_to_all | solution.py:106
Sparse Core Ops, SparseCore 0:
  150.2 54.6 all-reduce.2
where the time goes:
time: 271 us; the launch traced here: 270 us
  waiting for transfers between devices  84.3 us (31%)
  local copies, waits for them, and re-layouts  68.5 us (25%)
  loops' own time  33 us (12%)
  matrix products  30.9 us (11%)
  between operations  19.6 us (7%)
  starting transfers between devices  19.5 us (7%)
  other arithmetic  14.3 us (5%)
    psum x1, waiting for transfers between devices, body(): weighted, coverage = lax.psum((weighted, coverage), 'visit')  54.8 us
    another operation x1, loops' own time, body(): lax.fori_loop(0, buffer_slots, place_block, (empty, empty))  32.4 us
    gather x24, local copies, waits for them, and re-layouts  20.8 us
    dynamic_update_slice x8, local copies, waits for them, and re-layouts, place_block(): lax.dynamic_update_slice(coverage, region + block_weight, (corner_top, co...  14.4 us
    dynamic_update_slice x8, local copies, waits for them, and re-layouts, place_block(): lax.dynamic_update_slice(weighted, region + block_weight * arrived[positi...  14.4 us
    all_to_all x1, waiting for transfers between devices, body(): lax.all_to_all(cut_back, 'sky', split_axis=0, concat_axis=0, tiled=True)  13.8 us
    all_to_all x1, waiting for transfers between devices, body(): lax.all_to_all(packed, 'sky', split_axis=0, concat_axis=0, tiled=True)  11.1 us
    all_to_all x1, starting transfers between devices, body(): lax.all_to_all(sent_weight, 'sky', split_axis=0, concat_axis=0, tiled=True)  6.35 us
  transfers between devices with their start and end apart: 5, of which 4 were waited for; matrix products, arithmetic and copies ran while one was open for 9% of the time, Pallas kernels for 0%

commit v1 on v0

--- a/solution.py
+++ b/solution.py
@@ -9,6 +9,28 @@
 WIDTHS = (1.0, 1.0, 1.0, 2.5, 2.5, 2.5, 5.0)
 POWERS = (0, 1, 2, 0, 1, 2, 0)
 PRECISE = lax.Precision.HIGHEST
+
+
+def in_blocks(x, dim, length):
+    before, after = (x.shape[:dim], x.shape[dim + 1 :])
+    return jnp.moveaxis(x.reshape(*before, length, -1, *after), dim, 0)
+
+
+def in_order(blocks, dim):
+    shape = list(blocks.shape[1:])
+    shape[dim] *= blocks.shape[0]
+    return jnp.moveaxis(blocks, 0, dim).reshape(shape)
+
+
+def rotated_exchange(value, axis, split_dim, concat_dim):
+    size, here = (lax.axis_size(axis), lax.axis_index(axis))
+    parts = in_blocks(value, split_dim, size)
+    done = [parts[here]]
+    for step in range(1, size):
+        sent = parts[(here + step) % size]
+        done.append(lax.ppermute(sent, axis, [(i, (i + step) % size) for i in range(size)]))
+    parts = jnp.stack(done)[(here - jnp.arange(size)) % size]
+    return in_order(parts, concat_dim)
 
 
 def profile_filters(side):
@@ -75,7 +97,7 @@
     sent_weight = jnp.dot(routing, weight[0], precision=PRECISE)
     sent_corner = jnp.dot(routing, offsets[0].astype(jnp.float32), precision=PRECISE)
     arrived, arrived_weight, arrived_corner = (
-        lax.all_to_all(packed, "sky", split_axis=0, concat_axis=0, tiled=True),
+        rotated_exchange(packed, "sky", 0, 0),
         lax.all_to_all(sent_weight, "sky", split_axis=0, concat_axis=0, tiled=True),
         lax.all_to_all(sent_corner, "sky", split_axis=0, concat_axis=0, tiled=True),
     )

time: 271 us -> 262 us (0.967)
  waiting for transfers between devices: 84.3 us -> 77.8 us
    all_to_all x1 -> x0, waiting for transfers between devices: 11.1 us -> none  [body(): lax.all_to_all(packed, 'sky', split_axis=0, concat_axis=0, tiled=True)]
    ppermute x0 -> x3, starting transfers between devices: none -> 7.04 us  [rotated_exchange(): lax.ppermute(sent, axis, [(i, (i + step) % size) for i in range(size)])]
    all_to_all x1, waiting for transfers between devices: 0.01 us -> 5.04 us  [body(): lax.all_to_all(sent_weight, 'sky', split_axis=0, concat_axis=0, tiled=True)]
    all_to_all x1 -> x0, starting transfers between devices: 3.47 us -> none  [body(): lax.all_to_all(packed, 'sky', split_axis=0, concat_axis=0, tiled=True)]
    all_to_all x1, starting transfers between devices: 6.35 us -> 3.35 us  [body(): lax.all_to_all(sent_weight, 'sky', split_axis=0, concat_axis=0, tiled=True)]
    gather x24 -> x25, local copies, waits for them, and re-layouts: 20.8 us -> 21.4 us
  transfers between devices with their start and end apart: 5 -> 7, of which waited for: 4 -> 4; matrix products, arithmetic and copies ran while one was open for 9% -> 1% of each run, Pallas kernels for 0% -> 0%
where the time goes in v1:
time: 262 us; the launch traced here: 261 us
  waiting for transfers between devices  77.8 us (30%)
  local copies, waits for them, and re-layouts  67.9 us (26%)
  loops' own time  32 us (12%)
  matrix products  30.9 us (12%)
  between operations  19.7 us (8%)
  starting transfers between devices  18.2 us (7%)
  other arithmetic  14.8 us (6%)
    psum x1, waiting for transfers between devices, body(): weighted, coverage = lax.psum((weighted, coverage), 'visit')  54.8 us
    another operation x1, loops' own time, body(): lax.fori_loop(0, buffer_slots, place_block, (empty, empty))  31.4 us
    gather x24, local copies, waits for them, and re-layouts  20.8 us
    dynamic_update_slice x8, local copies, waits for them, and re-layouts, place_block(): lax.dynamic_update_slice(coverage, region + block_weight, (corner_top, co...  14.4 us
    dynamic_update_slice x8, local copies, waits for them, and re-layouts, place_block(): lax.dynamic_update_slice(weighted, region + block_weight * arrived[positi...  14.4 us
    all_to_all x1, waiting for transfers between devices, body(): lax.all_to_all(cut_back, 'sky', split_axis=0, concat_axis=0, tiled=True)  13.8 us
    ppermute x3, starting transfers between devices, rotated_exchange(): lax.ppermute(sent, axis, [(i, (i + step) % size) for i in range(size)])  7.04 us
    add x8, other arithmetic, place_block(): region + block_weight * arrived[position]  6.03 us
  transfers between devices with their start and end apart: 7, of which 4 were waited for; matrix products, arithmetic and copies ran while one was open for 1% of the time, Pallas kernels for 0%

profile of v1, /device:TPU:0, one launch (start us, length us, event | category | flops | bytes accessed | tf_op | source)
XLA Modules:
  0.0 261.4 jit_solution(12023912956948725001)
XLA Ops:
  17.9 0.9 copy-done.4
  18.8 15.7 %while.42 = (s32[]{:T(128)}, f32[4,128,128]{2,1,0:T(8,128)S(1)}, f32[4,3,49]{2,1,0:T(4,128)S(1)}, f32[7,128,128]{2,0,1:T(8,128)S(1)}, f32[4,128,128]{2,1,0:T(8,128)S(1)}, /*index=5*/s32[]{:T(128)}) while((s32[]{:T(128)}, f32[4,128,128]{2,1,0:T(8,128)S(1)}, f32[4,3,49]{2,1,0:T(4,128)S(1)}, ...), condition=%wide.region_10.11_spmd.clone.clone, body=%wide.region_9.10_spmd.clone.clone.sunk | while | flops 557646336 | bytes 6362725 | solution.py:84
  37.5 3.1 %collective-permute-start = (f32[2,128,128]{2,1,0:T(8,128)S(1)}, f32[2,128,128]{2,1,0:T(8,128)S(1)}, u32[]{:S(2)}, u32[]{:S(2)}) collective-permute-start(f32[2,128,128]{2,1,0:T(8,128)S(1)} %bitcast.217), channel_id=1, source_target_pairs={{0,1},{1,2},{2,3},{3,0},{4,5},{5,6},{6,7},{7,4},{8,9},{9,10},{10,1... | collective-permute-start | bytes 393224 | tf_op jit(solution)/shard_map/ppermute | solution.py:31
  40.6 2.6 collective-permute-start.1
  43.1 1.4 collective-permute-start.2
  45.4 3.4 %all-to-all-start.1 = ((f32[4,2,1]{1,2,0:T(1,128)}), f32[4,2,1]{1,2,0:T(1,128)S(1)}, u32[]{:S(2)}, u32[]{:S(2)}) async-start(f32[4,2,1]{1,2,0:T(1,128)} %copy.56), calls=%async_computation.1 | async-start | bytes 4096 | tf_op jit(solution)/shard_map/all_to_all | solution.py:101
  49.5 5.0 %all-to-all-done.1 = f32[4,2,1]{1,2,0:T(1,128)S(1)} async-done(((f32[4,2,1]{1,2,0:T(1,128)}), f32[4,2,1]{1,2,0:T(1,128)S(1)}, u32[]{:S(2)}, u32[]{:S(2)}) %all-to-all-start.1) | async-done | bytes 64 | tf_op jit(solution)/shard_map/all_to_all | solution.py:101
  54.6 3.2 %all-to-all-start = ((f32[4,2,2]{2,1,0:T(2,128)}), f32[4,2,2]{2,1,0:T(2,128)S(1)}, u32[]{:S(2)}, u32[]{:S(2)}) async-start(f32[4,2,2]{2,1,0:T(2,128)} %fusion.28), calls=%async_computation | async-start | bytes 8192 | tf_op jit(solution)/shard_map/all_to_all | solution.py:102
  59.1 4.2 %all-to-all-done = f32[4,2,2]{2,1,0:T(2,128)S(1)} async-done(((f32[4,2,2]{2,1,0:T(2,128)}), f32[4,2,2]{2,1,0:T(2,128)S(1)}, u32[]{:S(2)}, u32[]{:S(2)}) %all-to-all-start) | async-done | bytes 96 | tf_op jit(solution)/shard_map/all_to_all | solution.py:102
  64.8 75.6 %while.40 = (s32[]{:T(128)}, f32[256,256]{1,0:T(8,128)S(1)}, f32[256,256]{1,0:T(8,128)S(1)}, s32[8,2]{0,1:T(2,128)S(1)}, f32[8]{0:T(128)S(1)}, /*index=5*/f32[8,...) while((s32[]{:T(128)}, f32[256,256]{1,0:T(8,128)S(1)}, f32[256,256]{1,0:T(8,128)S(1)}, ...), condition=%wide.region_12.13_spmd, body=%wide.region_11.12_spmd.sunk | while | flops 49160 | bytes 591569 | solution.py:122
  69.9 0.8 bitcast_add_fusion.2
  70.7 2.0 dynamic_update_slice.32
  72.7 2.0 dynamic_update_slice.31
  79.7 0.8 bitcast_add_fusion.2
  80.5 1.9 dynamic_update_slice.32
  82.4 1.9 dynamic_update_slice.31
  89.5 0.8 bitcast_add_fusion.2
  90.2 2.0 dynamic_update_slice.32
  92.2 2.0 dynamic_update_slice.31
  99.2 0.8 bitcast_add_fusion.2
  100.0 1.7 dynamic_update_slice.32
  101.7 1.7 dynamic_update_slice.31
  108.4 0.8 bitcast_add_fusion.2
  109.2 1.9 dynamic_update_slice.32
  111.1 1.9 dynamic_update_slice.31
  118.0 0.8 bitcast_add_fusion.2
  118.8 1.7 dynamic_update_slice.32
  120.5 1.7 dynamic_update_slice.31
  127.2 0.8 bitcast_add_fusion.2
  128.0 1.7 dynamic_update_slice.32
  129.6 1.7 dynamic_update_slice.31
  137.1 1.7 dynamic_update_slice.32
  138.8 1.7 dynamic_update_slice.31
  141.3 54.8 %all-reduce.3.cloned.1.call-done = (f32[256,256]{1,0:T(8,128)}, f32[256,256]{1,0:T(8,128)}) async-done(((f32[256,256]{1,0:T(8,128)}, f32[256,256]{1,0:T(8,128)}), (f32[256,256]{1,0:T(8,128)}, f32[256,256]{1,0:T(8,128)})) %all-reduce.3.cloned.1.call-update) | async-done | bytes 524304 | tf_op jit(solution)/shard_map/psum | solution.py:123
  196.1 1.1 add_divide_fusion
  197.2 20.8 %while.41 = (s32[]{:T(128)}, f32[256,256]{1,0:T(8,128)S(1)}, s32[8,2]{0,1:T(2,128)S(1)}, f32[8,128,128]{2,1,0:T(8,128)}, s32[]{:T(128)}) while((s32[]{:T(128)}, f32[256,256]{1,0:T(8,128)S(1)}, s32[8,2]{0,1:T(2,128)S(1)}, f32[8,128,128]{2,1,0:T(8,128)}, s32[]{:T(128)}) %tuple.119), condition=%wide.while_cond, body=%wide.while_body.sunk | while | flops 2 | bytes 132705 | solution.py:126
  197.8 2.0 bitcast_dynamic-update-slice_fusion.2
  200.4 2.0 bitcast_dynamic-update-slice_fusion.2
  203.0 2.0 bitcast_dynamic-update-slice_fusion.2
  205.6 2.0 bitcast_dynamic-update-slice_fusion.2
  208.2 2.0 bitcast_dynamic-update-slice_fusion.2
  210.8 2.0 bitcast_dynamic-update-slice_fusion.2
  213.4 2.0 bitcast_dynamic-update-slice_fusion.2
  216.0 2.0 bitcast_dynamic-update-slice_fusion.2
  218.7 4.6 %all-to-all-start.2 = ((f32[8,128,128]{2,1,0:T(8,128)}), f32[8,128,128]{2,1,0:T(8,128)S(1)}, u32[]{:S(2)}, u32[]{:S(2)}) async-start(f32[8,128,128]{2,1,0:T(8,128)} %get-tuple-element.193), calls=%async_computation.2 | async-start | bytes 1048576 | tf_op jit(solution)/shard_map/all_to_all | solution.py:128
  223.2 13.8 %all-to-all-done.2 = f32[8,128,128]{2,1,0:T(8,128)S(1)} async-done(((f32[8,128,128]{2,1,0:T(8,128)}), f32[8,128,128]{2,1,0:T(8,128)S(1)}, u32[]{:S(2)}, u32[]{:S(2)}) %all-to-all-start.2) | async-done | bytes 524320 | tf_op jit(solution)/shard_map/all_to_all | solution.py:128
  237.7 16.0 %while.43 = (s32[]{:T(128)}, f32[4,128,128]{2,1,0:T(8,128)S(1)}, f32[4,3,49]{2,1,0:T(4,128)S(1)}, f32[7,128,128]{2,0,1:T(8,128)S(1)}, f32[4,128,128]{2,0,1:T(4,128)S(1)}, /*index=5*/s32[]{:T(128)}) while((s32[]{:T(128)}, f32[4,128,128]{2,1,0:T(8,128)S(1)}, f32[4,3,49]{2,1,0:T(4,128)S(1)}, ...), condition=%wide.region_16.17_spmd.clone.clone, body=%wide.region_15.16_spmd.clone.clone.sunk | while | flops 557646336 | bytes 6428261 | solution.py:132
  253.7 0.8 select_bitcast_fusion
  (200 shorter events, 60.8 us)
Async XLA Ops:
  7.2 37.3 %copy-start = (f32[1,4]{1,0:T(1,128)S(1)}, f32[1,4]{1,0:T(1,128)}, u32[]{:S(2)}) copy-start(f32[1,4]{1,0:T(1,128)} %param.17) | copy-start | bytes 52
  12.4 4.1 %copy-start.5 = (f32[1,4,3,49]{3,1,2,0:T(4,128)S(1)}, f32[1,4,3,49]{3,1,2,0:T(4,128)}, u32[]{:S(2)}) copy-start(f32[1,4,3,49]{3,1,2,0:T(4,128)} %param.15) | copy-start | bytes 7060
  17.9 1.0 copy-start.4
  35.2 0.7 copy-start.8
  35.3 0.7 copy-start.9
  37.5 26.2 %collective-permute-start = (f32[2,128,128]{2,1,0:T(8,128)S(1)}, f32[2,128,128]{2,1,0:T(8,128)S(1)}, u32[]{:S(2)}, u32[]{:S(2)}) collective-permute-start(f32[2,128,128]{2,1,0:T(8,128)S(1)} %bitcast.217), channel_id=1, source_target_pairs={{0,1},{1,2},{2,3},{3,0},{4,5},{5,6},{6,7},{7,4},{8,9},{9,10},{10,1... | collective-permute-start | bytes 393224 | tf_op jit(solution)/shard_map/ppermute | solution.py:31
  40.6 23.1 %collective-permute-start.1 = (f32[2,128,128]{2,1,0:T(8,128)S(1)}, f32[2,128,128]{2,1,0:T(8,128)S(1)}, u32[]{:S(2)}, u32[]{:S(2)}) collective-permute-start(f32[2,128,128]{2,1,0:T(8,128)S(1)} %bitcast.215), channel_id=1, source_target_pairs={{0,2},{1,3},{2,0},{3,1},{4,6},{5,7},{6,4},{7,5},{8,10},{9,11},{10,... | collective-permute-start | bytes 393224 | tf_op jit(solution)/shard_map/ppermute | solution.py:31
  43.1 20.5 %collective-permute-start.2 = (f32[2,128,128]{2,1,0:T(8,128)S(1)}, f32[2,128,128]{2,1,0:T(8,128)S(1)}, u32[]{:S(2)}, u32[]{:S(2)}) collective-permute-start(f32[2,128,128]{2,1,0:T(8,128)S(1)} %bitcast.214), channel_id=1, source_target_pairs={{0,3},{1,0},{2,1},{3,2},{4,7},{5,4},{6,5},{7,6},{8,11},{9,8},{10,9... | collective-permute-start | bytes 393224 | tf_op jit(solution)/shard_map/ppermute | solution.py:31
  45.4 3.4 %copy-start.7 = (s32[1,4,2]{1,2,0:T(2,128)S(1)}, s32[1,4,2]{1,2,0:T(2,128)}, u32[]{:S(2)}) copy-start(s32[1,4,2]{1,2,0:T(2,128)} %param.19) | copy-start | bytes 100
  45.4 9.2 %all-to-all-start.1 = ((f32[4,2,1]{1,2,0:T(1,128)}), f32[4,2,1]{1,2,0:T(1,128)S(1)}, u32[]{:S(2)}, u32[]{:S(2)}) async-start(f32[4,2,1]{1,2,0:T(1,128)} %copy.56), calls=%async_computation.1 | async-start | bytes 4096 | tf_op jit(solution)/shard_map/all_to_all | solution.py:101
  54.6 8.8 %all-to-all-start = ((f32[4,2,2]{2,1,0:T(2,128)}), f32[4,2,2]{2,1,0:T(2,128)S(1)}, u32[]{:S(2)}, u32[]{:S(2)}) async-start(f32[4,2,2]{2,1,0:T(2,128)} %fusion.28), calls=%async_computation | async-start | bytes 8192 | tf_op jit(solution)/shard_map/all_to_all | solution.py:102
  57.8 138.3 %all-reduce.3.cloned.1.call-start = ((), (), s32[]{:S(2)}) async-start(), calls=%async_computation.3 | async-start | bytes 1048576 | tf_op jit(solution)/shard_map/psum | solution.py:123
  140.5 0.7 copy-start.1
  140.5 0.8 copy-start.2
  218.0 0.7 copy-start.3
  218.0 5.3 %copy-start.6 = (f32[1,4,3,49]{3,1,2,0:T(4,128)S(1)}, f32[1,4,3,49]{3,1,2,0:T(4,128)}, u32[]{:S(2)}) copy-start(f32[1,4,3,49]{3,1,2,0:T(4,128)} %param.16) | copy-start | bytes 7060
  218.7 18.3 %all-to-all-start.2 = ((f32[8,128,128]{2,1,0:T(8,128)}), f32[8,128,128]{2,1,0:T(8,128)S(1)}, u32[]{:S(2)}, u32[]{:S(2)}) async-start(f32[8,128,128]{2,1,0:T(8,128)} %get-tuple-element.193), calls=%async_computation.2 | async-start | bytes 1048576 | tf_op jit(solution)/shard_map/all_to_all | solution.py:128
Sparse Core Ops, SparseCore 0:
  141.4 54.6 all-reduce.2
